TPU v7x, 32 devices: a whole 2x2x4 slice. The times are simulated.
32 devices in a mesh: dp: 8 (over y, x, core), mp: 4 (over z).
Axes of the slice: x: 2, y: 2, z: 4, core: 2. Of those that a mesh axis runs over, the one named last changes fastest.
Arguments:
- tokens: bfloat16 [8192, 2048], P(('dp', 'mp')), may hold values from -6 to 6
- valid: int32 [8], P('dp'), may hold values from 256 to 1024, as said below
- attn_gain: float32 [2048], replicated, may hold values from 0.25 to 1.75
- w_query: bfloat16 [2048, 2048], replicated, may hold values from -0.125 to 0.125
- w_key: bfloat16 [2048, 2048], replicated, may hold values from -0.125 to 0.125
- w_value: bfloat16 [2048, 2048], replicated, may hold values from -0.125 to 0.125
- w_rank: bfloat16 [2048, 16], replicated, may hold values from -0.125 to 0.125
- w_forget: bfloat16 [16, 256], replicated, may hold values from -1.5 to 1.5
- forget_bias: float32 [256], replicated, may hold values from -2 to 6
- head_gain: float32 [512], replicated, may hold values from 0.25 to 1.75
- w_out: bfloat16 [2048, 2048], replicated, may hold values from -0.125 to 0.125
- mlp_gain: float32 [2048], replicated, may hold values from 0.25 to 1.75
- w_gate: bfloat16 [2048, 5632], P(None, 'mp'), may hold values from -0.125 to 0.125
- w_up: bfloat16 [2048, 5632], P(None, 'mp'), may hold values from -0.125 to 0.125
- w_down: bfloat16 [5632, 2048], P('mp'), may hold values from -0.15625 to 0.15625
- cotangent: bfloat16 [8192, 2048], P(('dp', 'mp')), may hold values from -6 to 6
Outputs:
- output: bfloat16 [8192, 2048], P(('dp', 'mp'))
- grad_tokens: float32 [8192, 2048], P(('dp', 'mp'))
- grad_attn_gain: float32 [2048], P('dp')
- grad_query: float32 [2048, 2048], P('dp', 'mp')
- grad_key: float32 [2048, 2048], P('dp', 'mp')
- grad_value: float32 [2048, 2048], P('dp', 'mp')
- grad_rank: float32 [2048, 16], P('dp')
- grad_forget: float32 [16, 256], P(None, 'dp')
- grad_forget_bias: float32 [256], P('dp')
- grad_head_gain: float32 [512], P('dp')
- grad_out: float32 [2048, 2048], P('dp', 'mp')
- grad_mlp_gain: float32 [2048], P('dp')
- grad_gate: float32 [2048, 5632], P('dp', 'mp')
- grad_up: float32 [2048, 5632], P('dp', 'mp')
- grad_down: float32 [5632, 2048], P('mp', 'dp')
Inputs may be any that keep to these rules, and one draw needn't show every extreme that they name: Each bucket holds one sequence whose first valid tokens count; one bucket is full in every draw.
All inputs are finite; a program needn't handle non-finite values.
Results may differ from a plain program's by a relative error of at most 0.018.
Values may be sent and summed in bfloat16 or wider, within the bound.
No kernel may reach another device: no remote copies, remote signals or barrier semaphores. Data moves between devices by JAX's collectives and lax.ppermute only.
A program may use at most 448 MiB of HBM per device.

v0:
```python
import math
import jax
import jax.numpy as jnp
from jax import lax
from jax.sharding import PartitionSpec as P

HEADS = 4
BLOCK = 128
EPS = 1e-06
GATE_NORM = 8.0
HIGH_PRECISION = lax.Precision.HIGHEST
CONTRACT_ROWS = (((0,), (0,)), ((), ()))
CONTRACT_COLS = (((1,), (1,)), ((), ()))


def rms_norm(values, gain):
    return values * lax.rsqrt(jnp.mean(values * values, axis=-1, keepdims=True) + EPS) * gain


def silu_slope(raw):
    sigmoid = jax.nn.sigmoid(raw)
    return sigmoid * (1.0 + raw * (1.0 - sigmoid))


def rows_product(left, right):
    return lax.dot_general(left, right, CONTRACT_ROWS, preferred_element_type=jnp.float32)


def cols_product(left, right):
    return lax.dot_general(left, right, CONTRACT_COLS, preferred_element_type=jnp.float32)


def piece_step(states, block):
    key_slot_state, value_slot_state = states
    query_rows, key_row_block, value_row_block, log_decay = block
    length = query_rows.shape[0]
    scale = 1.0 / math.sqrt(query_rows.shape[2])
    running_total = jnp.cumsum(log_decay, axis=0)
    fresh = 1.0 - jnp.exp(log_decay)
    causal = (jnp.arange(length)[:, None] >= jnp.arange(length)[None, :])[:, :, None, None]
    spread = running_total[:, None] - running_total[None, :]
    weights = jnp.where(causal, jnp.exp(jnp.where(causal, spread, 0.0)), 0.0) * fresh[None]
    direct = jnp.einsum("thd,jhd->htj", query_rows, key_row_block, precision=HIGH_PRECISION)
    attention_scores = jnp.exp(running_total) * jnp.einsum(
        "cso,sio->csi", query_rows, key_slot_state, precision=HIGH_PRECISION
    )
    attention_scores = (
        attention_scores + jnp.einsum("htj,tjhm->thm", direct, weights, precision=HIGH_PRECISION)
    ) * scale
    attention_probabilities = jax.nn.softmax(attention_scores, axis=-1)
    mixing = jnp.einsum("thm,tjhm->htj", attention_probabilities, weights, precision=HIGH_PRECISION)
    output_rows = jnp.einsum(
        "lwe,wez->lwz",
        attention_probabilities * jnp.exp(running_total),
        value_slot_state,
        precision=HIGH_PRECISION,
    )
    output_rows = output_rows + jnp.einsum(
        "htj,jhd->thd", mixing, value_row_block, precision=HIGH_PRECISION
    )
    final = running_total[-1]
    carried_state = jnp.exp(final[None] - running_total) * fresh
    key_slot_state = jnp.exp(final)[:, :, None] * key_slot_state + jnp.einsum(
        "eoq,eon->oqn", carried_state, key_row_block, precision=HIGH_PRECISION
    )
    value_slot_state = jnp.exp(final)[:, :, None] * value_slot_state + jnp.einsum(
        "eoq,eon->oqn", carried_state, value_row_block, precision=HIGH_PRECISION
    )
    return ((key_slot_state, value_slot_state), output_rows)


def slot_block(states, block):
    length = block[0].shape[0]
    piece_length = min(16, length)
    count = length // piece_length
    pieces = tuple((member.reshape((count, piece_length) + member.shape[1:]) for member in block))
    states, output_rows = lax.scan(piece_step, states, pieces)
    return (states, output_rows.reshape(block[0].shape))


def slot_mixer(query_rows, key_row_block, value_row_block, log_decay):
    steps = query_rows.shape[0] // BLOCK
    blocks = tuple(
        (
            member.reshape((steps, BLOCK) + member.shape[1:])
            for member in (query_rows, key_row_block, value_row_block, log_decay)
        )
    )
    blank_state = jnp.zeros(
        (query_rows.shape[1], log_decay.shape[2], query_rows.shape[2]), jnp.float32
    )
    _, output_rows = lax.scan(jax.checkpoint(slot_block), (blank_state, blank_state), blocks)
    return output_rows.reshape(query_rows.shape)


def local(
    tokens,
    valid,
    attn_gain,
    w_query,
    w_key,
    w_value,
    w_rank,
    w_forget,
    forget_bias,
    head_gain,
    w_out,
    mlp_gain,
    w_gate,
    w_up,
    w_down,
    cotangent,
):
    shard_rows = tokens.shape[0]
    gathered, upstream = (
        lax.all_gather(tokens, "mp", axis=0, tiled=True),
        lax.all_gather(cotangent, "mp", axis=0, tiled=True),
    )
    group_len = gathered.shape[0]
    model_width = w_query.shape[0]
    head_size = model_width // HEADS
    slot_count = forget_bias.shape[0] // HEADS
    shard_index = lax.axis_index("mp")
    column_width = model_width // lax.axis_size("mp")
    own_begin = shard_index * shard_rows
    valid_mask = (jnp.arange(group_len) < valid[0]).astype(jnp.float32)[:, None]
    resid = gathered.astype(jnp.float32)
    normed, pull_first = jax.vjp(rms_norm, resid, attn_gain)
    normed_low = normed.astype(jnp.bfloat16)
    query_raw = jnp.dot(normed_low, w_query, preferred_element_type=jnp.float32)
    key_raw = jnp.dot(normed_low, w_key, preferred_element_type=jnp.float32)
    value_raw = jnp.dot(normed_low, w_value, preferred_element_type=jnp.float32)
    rank_rows = jnp.dot(normed_low, w_rank, preferred_element_type=jnp.float32)
    forget_dense = w_forget.astype(jnp.float32)
    logits = jnp.dot(rank_rows, forget_dense, precision=HIGH_PRECISION) + forget_bias
    log_decay = jax.nn.log_sigmoid(logits) / GATE_NORM

    def heads_view(values, inner_width):
        return values.astype(jnp.float32).reshape(group_len, HEADS, inner_width)

    mixed, pull_slots = jax.vjp(
        slot_mixer,
        heads_view(jax.nn.silu(query_raw).astype(jnp.bfloat16), head_size),
        heads_view(jax.nn.silu(key_raw).astype(jnp.bfloat16), head_size),
        heads_view(value_raw.astype(jnp.bfloat16), head_size),
        heads_view(log_decay, slot_count),
    )
    head_normed, pull_head = jax.vjp(rms_norm, mixed, head_gain)
    head_low = head_normed.reshape(group_len, model_width).astype(jnp.bfloat16)
    hidden_res = resid + jnp.dot(head_low, w_out, preferred_element_type=jnp.float32)
    normed_mlp, pull_second = jax.vjp(rms_norm, hidden_res, mlp_gain)
    mlp_low = normed_mlp.astype(jnp.bfloat16)
    gate_pre = jnp.dot(mlp_low, w_gate, preferred_element_type=jnp.float32)
    up_pre = jnp.dot(mlp_low, w_up, preferred_element_type=jnp.float32)
    activated = jax.nn.silu(gate_pre)
    inner_low = (activated * up_pre).astype(jnp.bfloat16)
    mlp_own = lax.psum_scatter(
        jnp.dot(inner_low, w_down, preferred_element_type=jnp.float32).astype(jnp.bfloat16),
        "mp",
        scatter_dimension=0,
        tiled=True,
    ).astype(jnp.float32)
    own_mask = lax.dynamic_slice_in_dim(valid_mask, own_begin, shard_rows, 0)
    own_hidden = lax.dynamic_slice_in_dim(hidden_res, own_begin, shard_rows, 0)
    output = ((own_hidden + mlp_own) * own_mask).astype(jnp.bfloat16)
    grad_output = upstream.astype(jnp.float32) * valid_mask
    grad_out_low = grad_output.astype(jnp.bfloat16)
    grad_down = rows_product(inner_low, grad_out_low)
    grad_inner = cols_product(grad_out_low, w_down)
    grad_gate_low = (grad_inner * up_pre * silu_slope(gate_pre)).astype(jnp.bfloat16)
    grad_up_low = (grad_inner * activated).astype(jnp.bfloat16)
    grad_gate = rows_product(mlp_low, grad_gate_low)
    grad_up = rows_product(mlp_low, grad_up_low)
    partial_grad = cols_product(grad_gate_low, w_gate) + cols_product(grad_up_low, w_up)
    grad_normed_mlp = lax.psum(partial_grad, "mp")
    grad_res_mlp, grad_mlp_gain = pull_second(grad_normed_mlp)
    grad_hidden = grad_output + grad_res_mlp

    def own_columns(values):
        return lax.dynamic_slice_in_dim(values, shard_index * column_width, column_width, 1)

    grad_hidden_low = grad_hidden.astype(jnp.bfloat16)
    grad_wout = rows_product(head_low, own_columns(grad_hidden_low))
    grad_head_flat = cols_product(grad_hidden_low, w_out)
    grad_mixed, grad_head_gain = pull_head(grad_head_flat.reshape(group_len, HEADS, head_size))
    grad_query_in, grad_key_in, grad_value_in, grad_log_in = pull_slots(grad_mixed)
    grad_query_low = (grad_query_in.reshape(group_len, model_width) * silu_slope(query_raw)).astype(
        jnp.bfloat16
    )
    grad_key_low = (grad_key_in.reshape(group_len, model_width) * silu_slope(key_raw)).astype(
        jnp.bfloat16
    )
    grad_value_low = grad_value_in.reshape(group_len, model_width).astype(jnp.bfloat16)
    grad_logits = (
        grad_log_in.reshape(group_len, HEADS * slot_count) * jax.nn.sigmoid(-logits) / GATE_NORM
    )
    grad_bias = jnp.sum(grad_logits, axis=0)
    grad_forget = lax.dot_general(
        rank_rows,
        grad_logits,
        CONTRACT_ROWS,
        precision=HIGH_PRECISION,
        preferred_element_type=jnp.float32,
    )
    grad_rank_low = lax.dot_general(
        grad_logits,
        forget_dense,
        CONTRACT_COLS,
        precision=HIGH_PRECISION,
        preferred_element_type=jnp.float32,
    ).astype(jnp.bfloat16)
    grad_wrank = rows_product(normed_low, grad_rank_low)
    grad_wquery = rows_product(normed_low, own_columns(grad_query_low))
    grad_wkey = rows_product(normed_low, own_columns(grad_key_low))
    grad_wvalue = rows_product(normed_low, own_columns(grad_value_low))
    grad_normed = cols_product(grad_query_low, w_query) + cols_product(grad_key_low, w_key)
    grad_normed = (
        grad_normed + cols_product(grad_value_low, w_value) + cols_product(grad_rank_low, w_rank)
    )
    grad_resid, grad_attn_gain = pull_first(grad_normed)
    grad_tokens = lax.dynamic_slice_in_dim(grad_hidden + grad_resid, own_begin, shard_rows, 0)
    (
        sum_query,
        sum_key,
        sum_value,
        sum_rank,
        sum_forget,
        sum_bias,
        sum_head_gain,
        sum_wout,
        sum_attn_gain,
        sum_gate,
        sum_up,
        sum_down,
        sum_mlp_gain,
    ) = (
        lax.psum_scatter(grad_wquery, "dp", scatter_dimension=0, tiled=True),
        lax.psum_scatter(grad_wkey, "dp", scatter_dimension=0, tiled=True),
        lax.psum_scatter(grad_wvalue, "dp", scatter_dimension=0, tiled=True),
        lax.psum_scatter(grad_wrank, "dp", scatter_dimension=0, tiled=True),
        lax.psum_scatter(grad_forget, "dp", scatter_dimension=1, tiled=True),
        lax.psum_scatter(grad_bias, "dp", scatter_dimension=0, tiled=True),
        lax.psum_scatter(grad_head_gain, "dp", scatter_dimension=0, tiled=True),
        lax.psum_scatter(grad_wout, "dp", scatter_dimension=0, tiled=True),
        lax.psum_scatter(grad_attn_gain, "dp", scatter_dimension=0, tiled=True),
        lax.psum_scatter(grad_gate, "dp", scatter_dimension=0, tiled=True),
        lax.psum_scatter(grad_up, "dp", scatter_dimension=0, tiled=True),
        lax.psum_scatter(grad_down, "dp", scatter_dimension=1, tiled=True),
        lax.psum_scatter(grad_mlp_gain, "dp", scatter_dimension=0, tiled=True),
    )
    return (
        output,
        grad_tokens,
        sum_attn_gain,
        sum_query,
        sum_key,
        sum_value,
        sum_rank,
        sum_forget,
        sum_bias,
        sum_head_gain,
        sum_wout,
        sum_mlp_gain,
        sum_gate,
        sum_up,
        sum_down,
    )


def solution(mesh):
    return jax.shard_map(
        local,
        mesh=mesh,
        in_specs=(
            P(("dp", "mp"), None),
            P("dp"),
            P(),
            P(),
            P(),
            P(),
            P(),
            P(),
            P(),
            P(),
            P(),
            P(),
            P(None, "mp"),
            P(None, "mp"),
            P("mp", None),
            P(("dp", "mp"), None),
        ),
        out_specs=(
            P(("dp", "mp"), None),
            P(("dp", "mp"), None),
            P("dp"),
            P("dp", "mp"),
            P("dp", "mp"),
            P("dp", "mp"),
            P("dp", None),
            P(None, "dp"),
            P("dp"),
            P("dp"),
            P("dp", "mp"),
            P("dp"),
            P("dp", "mp"),
            P("dp", "mp"),
            P("mp", "dp"),
        ),
        check_vma=False,
    )
```

profile of v0, /device:TPU:0, one launch (start us, length us, event | category | flops | bytes accessed | tf_op | source)
XLA Modules:
  0.0 5010.8 jit_solution(17685367575077738761)
XLA Ops:
  11.3 81.7 %all-gather.3.cloned.1.call-done = bf16[1024,2048]{1,0:T(8,128)(2,1)} async-done(((bf16[256,2048]{1,0:T(8,128)(2,1)}), bf16[1024,2048]{1,0:T(8,128)(2,1)}) %all-gather.3.cloned.1.call-update) | async-done | bytes 4194320 | tf_op jit(solution)/shard_map/all_gather | solution.py:116
  104.5 17.5 fusion.173
  142.2 15.3 fusion.174
  177.9 13.3 convert_convert_fusion
  217.7 780.5 %while.238 = (s32[]{:T(128)}, f32[4,64,512]{2,1,0:T(8,128)}, f32[4,64,512]{2,1,0:T(8,128)}, f32[8,128,4,512]{3,2,1,0:T(4,128)}, f32[8,4,64,512]{3,2,1,0:T(8,128)...) while((s32[]{:T(128)}, f32[4,64,512]{2,1,0:T(8,128)}, ...), condition=%wide.region_7.8_spmd.clone.clone, body=%wide.region_1.7_spmd.clone.clone.sunk | while | flops 115744832 | bytes 20931168 | solution.py:92
  226.3 83.2 %while.241 = (s32[]{:T(128)}, f32[4,64,512]{2,1,0:T(8,128)S(1)}, f32[4,64,512]{2,1,0:T(8,128)S(1)}, f32[8,16,4,512]{3,2,1,0:T(4,128)}, f32[8,16,4,64]{3,2,1,0:T(...) while((s32[]{:T(128)}, f32[4,64,512]{2,1,0:T(8,128)S(1)}, ...), condition=%wide.region_6.6_spmd.clone, body=%wide.region_2.5_spmd.clone.sunk | while | flops 115744832 | bytes 5921913 | solution.py:77
  323.8 83.2 %while.241 = (s32[]{:T(128)}, f32[4,64,512]{2,1,0:T(8,128)S(1)}, f32[4,64,512]{2,1,0:T(8,128)S(1)}, f32[8,16,4,512]{3,2,1,0:T(4,128)}, f32[8,16,4,64]{3,2,1,0:T(...) while((s32[]{:T(128)}, f32[4,64,512]{2,1,0:T(8,128)S(1)}, ...), condition=%wide.region_6.6_spmd.clone, body=%wide.region_2.5_spmd.clone.sunk | while | flops 115744832 | bytes 5921913 | solution.py:77
  421.2 83.2 %while.241 = (s32[]{:T(128)}, f32[4,64,512]{2,1,0:T(8,128)S(1)}, f32[4,64,512]{2,1,0:T(8,128)S(1)}, f32[8,16,4,512]{3,2,1,0:T(4,128)}, f32[8,16,4,64]{3,2,1,0:T(...) while((s32[]{:T(128)}, f32[4,64,512]{2,1,0:T(8,128)S(1)}, ...), condition=%wide.region_6.6_spmd.clone, body=%wide.region_2.5_spmd.clone.sunk | while | flops 115744832 | bytes 5921913 | solution.py:77
  518.7 83.2 %while.241 = (s32[]{:T(128)}, f32[4,64,512]{2,1,0:T(8,128)S(1)}, f32[4,64,512]{2,1,0:T(8,128)S(1)}, f32[8,16,4,512]{3,2,1,0:T(4,128)}, f32[8,16,4,64]{3,2,1,0:T(...) while((s32[]{:T(128)}, f32[4,64,512]{2,1,0:T(8,128)S(1)}, ...), condition=%wide.region_6.6_spmd.clone, body=%wide.region_2.5_spmd.clone.sunk | while | flops 115744832 | bytes 5921913 | solution.py:77
  616.2 83.2 %while.241 = (s32[]{:T(128)}, f32[4,64,512]{2,1,0:T(8,128)S(1)}, f32[4,64,512]{2,1,0:T(8,128)S(1)}, f32[8,16,4,512]{3,2,1,0:T(4,128)}, f32[8,16,4,64]{3,2,1,0:T(...) while((s32[]{:T(128)}, f32[4,64,512]{2,1,0:T(8,128)S(1)}, ...), condition=%wide.region_6.6_spmd.clone, body=%wide.region_2.5_spmd.clone.sunk | while | flops 115744832 | bytes 5921913 | solution.py:77
  713.7 83.2 %while.241 = (s32[]{:T(128)}, f32[4,64,512]{2,1,0:T(8,128)S(1)}, f32[4,64,512]{2,1,0:T(8,128)S(1)}, f32[8,16,4,512]{3,2,1,0:T(4,128)}, f32[8,16,4,64]{3,2,1,0:T(...) while((s32[]{:T(128)}, f32[4,64,512]{2,1,0:T(8,128)S(1)}, ...), condition=%wide.region_6.6_spmd.clone, body=%wide.region_2.5_spmd.clone.sunk | while | flops 115744832 | bytes 5921913 | solution.py:77
  811.2 83.2 %while.241 = (s32[]{:T(128)}, f32[4,64,512]{2,1,0:T(8,128)S(1)}, f32[4,64,512]{2,1,0:T(8,128)S(1)}, f32[8,16,4,512]{3,2,1,0:T(4,128)}, f32[8,16,4,64]{3,2,1,0:T(...) while((s32[]{:T(128)}, f32[4,64,512]{2,1,0:T(8,128)S(1)}, ...), condition=%wide.region_6.6_spmd.clone, body=%wide.region_2.5_spmd.clone.sunk | while | flops 115744832 | bytes 5921913 | solution.py:77
  908.8 83.2 %while.241 = (s32[]{:T(128)}, f32[4,64,512]{2,1,0:T(8,128)S(1)}, f32[4,64,512]{2,1,0:T(8,128)S(1)}, f32[8,16,4,512]{3,2,1,0:T(4,128)}, f32[8,16,4,64]{3,2,1,0:T(...) while((s32[]{:T(128)}, f32[4,64,512]{2,1,0:T(8,128)S(1)}, ...), condition=%wide.region_6.6_spmd.clone, body=%wide.region_2.5_spmd.clone.sunk | while | flops 115744832 | bytes 5921913 | solution.py:77
  1020.1 11.9 mul.733
  1032.0 14.3 multiply_reduce_fusion.6
  1070.7 16.2 multiply_convert_fusion.7
  1111.7 11.6 convolution_convert_fusion
  1123.4 274.7 %all-reduce.8.cloned.1.call-done = f32[1024,2048]{1,0:T(8,128)} async-done(((f32[1024,2048]{1,0:T(8,128)}), f32[1024,2048]{1,0:T(8,128)}) %all-reduce.8.cloned.1.call-update) | async-done | bytes 8388624 | tf_op jit(solution)/shard_map/psum | solution.py:175
  1417.2 15.2 multiply_reduce_fusion.1
  1473.6 2958.0 %while.236 = (s32[]{:T(128)}, f32[4,64,512]{2,1,0:T(8,128)S(1)}, f32[4,64,512]{2,1,0:T(8,128)S(1)}, f32[8,128,4,512]{3,2,1,0:T(4,128)}, f32[8,128,4,512]{3,2,1,0...) while((s32[]{:T(128)}, f32[4,64,512]{2,1,0:T(8,128)S(1)}, ...), condition=%wide.region_30.31_spmd, body=%wide.region_14.0_spmd.sunk | while | flops 314950080 | bytes 50768096 | solution.py:92
  1489.9 117.2 %while.239 = (s32[]{:T(128)}, f32[4,64,512]{2,1,0:T(8,128)S(1)}, f32[4,64,512]{2,1,0:T(8,128)S(1)}, f32[8,4,64]{2,1,0:T(4,128)S(1)}, f32[8,4,64,512]{3,2,1,0:T(8...) while((s32[]{:T(128)}, f32[4,64,512]{2,1,0:T(8,128)S(1)}, ...), condition=%wide.region_19.19_spmd.clone.clone, body=%wide.region_15.18_spmd.clone.clone.sunk | while | flops 84529344 | bytes 8700445 | solution.py:77
  1610.3 227.5 %while.240 = (s32[]{:T(128)}, f32[4,64,512]{2,1,0:T(8,128)S(1)}, f32[4,64,512]{2,1,0:T(8,128)S(1)}, f32[8,16,4,512]{3,2,1,0:T(4,128)}, f32[8,16,4,512]{3,2,1,0:T...) while((s32[]{:T(128)}, f32[4,64,512]{2,1,0:T(8,128)S(1)}, ...), condition=%wide.region_29.29_spmd.clone.clone, body=%wide.region_20.28_spmd.clone.clone.sunk | while | flops 230158336 | bytes 13886109 | solution.py:77
  1859.6 117.2 %while.239 = (s32[]{:T(128)}, f32[4,64,512]{2,1,0:T(8,128)S(1)}, f32[4,64,512]{2,1,0:T(8,128)S(1)}, f32[8,4,64]{2,1,0:T(4,128)S(1)}, f32[8,4,64,512]{3,2,1,0:T(8...) while((s32[]{:T(128)}, f32[4,64,512]{2,1,0:T(8,128)S(1)}, ...), condition=%wide.region_19.19_spmd.clone.clone, body=%wide.region_15.18_spmd.clone.clone.sunk | while | flops 84529344 | bytes 8700445 | solution.py:77
  1980.0 227.5 %while.240 = (s32[]{:T(128)}, f32[4,64,512]{2,1,0:T(8,128)S(1)}, f32[4,64,512]{2,1,0:T(8,128)S(1)}, f32[8,16,4,512]{3,2,1,0:T(4,128)}, f32[8,16,4,512]{3,2,1,0:T...) while((s32[]{:T(128)}, f32[4,64,512]{2,1,0:T(8,128)S(1)}, ...), condition=%wide.region_29.29_spmd.clone.clone, body=%wide.region_20.28_spmd.clone.clone.sunk | while | flops 230158336 | bytes 13886109 | solution.py:77
  2229.3 117.2 %while.239 = (s32[]{:T(128)}, f32[4,64,512]{2,1,0:T(8,128)S(1)}, f32[4,64,512]{2,1,0:T(8,128)S(1)}, f32[8,4,64]{2,1,0:T(4,128)S(1)}, f32[8,4,64,512]{3,2,1,0:T(8...) while((s32[]{:T(128)}, f32[4,64,512]{2,1,0:T(8,128)S(1)}, ...), condition=%wide.region_19.19_spmd.clone.clone, body=%wide.region_15.18_spmd.clone.clone.sunk | while | flops 84529344 | bytes 8700445 | solution.py:77
  2349.8 227.5 %while.240 = (s32[]{:T(128)}, f32[4,64,512]{2,1,0:T(8,128)S(1)}, f32[4,64,512]{2,1,0:T(8,128)S(1)}, f32[8,16,4,512]{3,2,1,0:T(4,128)}, f32[8,16,4,512]{3,2,1,0:T...) while((s32[]{:T(128)}, f32[4,64,512]{2,1,0:T(8,128)S(1)}, ...), condition=%wide.region_29.29_spmd.clone.clone, body=%wide.region_20.28_spmd.clone.clone.sunk | while | flops 230158336 | bytes 13886109 | solution.py:77
  2599.0 117.2 %while.239 = (s32[]{:T(128)}, f32[4,64,512]{2,1,0:T(8,128)S(1)}, f32[4,64,512]{2,1,0:T(8,128)S(1)}, f32[8,4,64]{2,1,0:T(4,128)S(1)}, f32[8,4,64,512]{3,2,1,0:T(8...) while((s32[]{:T(128)}, f32[4,64,512]{2,1,0:T(8,128)S(1)}, ...), condition=%wide.region_19.19_spmd.clone.clone, body=%wide.region_15.18_spmd.clone.clone.sunk | while | flops 84529344 | bytes 8700445 | solution.py:77
  2719.4 227.5 %while.240 = (s32[]{:T(128)}, f32[4,64,512]{2,1,0:T(8,128)S(1)}, f32[4,64,512]{2,1,0:T(8,128)S(1)}, f32[8,16,4,512]{3,2,1,0:T(4,128)}, f32[8,16,4,512]{3,2,1,0:T...) while((s32[]{:T(128)}, f32[4,64,512]{2,1,0:T(8,128)S(1)}, ...), condition=%wide.region_29.29_spmd.clone.clone, body=%wide.region_20.28_spmd.clone.clone.sunk | while | flops 230158336 | bytes 13886109 | solution.py:77
  2968.7 117.2 %while.239 = (s32[]{:T(128)}, f32[4,64,512]{2,1,0:T(8,128)S(1)}, f32[4,64,512]{2,1,0:T(8,128)S(1)}, f32[8,4,64]{2,1,0:T(4,128)S(1)}, f32[8,4,64,512]{3,2,1,0:T(8...) while((s32[]{:T(128)}, f32[4,64,512]{2,1,0:T(8,128)S(1)}, ...), condition=%wide.region_19.19_spmd.clone.clone, body=%wide.region_15.18_spmd.clone.clone.sunk | while | flops 84529344 | bytes 8700445 | solution.py:77
  3089.1 227.5 %while.240 = (s32[]{:T(128)}, f32[4,64,512]{2,1,0:T(8,128)S(1)}, f32[4,64,512]{2,1,0:T(8,128)S(1)}, f32[8,16,4,512]{3,2,1,0:T(4,128)}, f32[8,16,4,512]{3,2,1,0:T...) while((s32[]{:T(128)}, f32[4,64,512]{2,1,0:T(8,128)S(1)}, ...), condition=%wide.region_29.29_spmd.clone.clone, body=%wide.region_20.28_spmd.clone.clone.sunk | while | flops 230158336 | bytes 13886109 | solution.py:77
  3338.3 117.2 %while.239 = (s32[]{:T(128)}, f32[4,64,512]{2,1,0:T(8,128)S(1)}, f32[4,64,512]{2,1,0:T(8,128)S(1)}, f32[8,4,64]{2,1,0:T(4,128)S(1)}, f32[8,4,64,512]{3,2,1,0:T(8...) while((s32[]{:T(128)}, f32[4,64,512]{2,1,0:T(8,128)S(1)}, ...), condition=%wide.region_19.19_spmd.clone.clone, body=%wide.region_15.18_spmd.clone.clone.sunk | while | flops 84529344 | bytes 8700445 | solution.py:77
  3458.7 227.5 %while.240 = (s32[]{:T(128)}, f32[4,64,512]{2,1,0:T(8,128)S(1)}, f32[4,64,512]{2,1,0:T(8,128)S(1)}, f32[8,16,4,512]{3,2,1,0:T(4,128)}, f32[8,16,4,512]{3,2,1,0:T...) while((s32[]{:T(128)}, f32[4,64,512]{2,1,0:T(8,128)S(1)}, ...), condition=%wide.region_29.29_spmd.clone.clone, body=%wide.region_20.28_spmd.clone.clone.sunk | while | flops 230158336 | bytes 13886109 | solution.py:77
  3708.0 117.2 %while.239 = (s32[]{:T(128)}, f32[4,64,512]{2,1,0:T(8,128)S(1)}, f32[4,64,512]{2,1,0:T(8,128)S(1)}, f32[8,4,64]{2,1,0:T(4,128)S(1)}, f32[8,4,64,512]{3,2,1,0:T(8...) while((s32[]{:T(128)}, f32[4,64,512]{2,1,0:T(8,128)S(1)}, ...), condition=%wide.region_19.19_spmd.clone.clone, body=%wide.region_15.18_spmd.clone.clone.sunk | while | flops 84529344 | bytes 8700445 | solution.py:77
  3828.4 227.5 %while.240 = (s32[]{:T(128)}, f32[4,64,512]{2,1,0:T(8,128)S(1)}, f32[4,64,512]{2,1,0:T(8,128)S(1)}, f32[8,16,4,512]{3,2,1,0:T(4,128)}, f32[8,16,4,512]{3,2,1,0:T...) while((s32[]{:T(128)}, f32[4,64,512]{2,1,0:T(8,128)S(1)}, ...), condition=%wide.region_29.29_spmd.clone.clone, body=%wide.region_20.28_spmd.clone.clone.sunk | while | flops 230158336 | bytes 13886109 | solution.py:77
  4077.7 117.2 %while.239 = (s32[]{:T(128)}, f32[4,64,512]{2,1,0:T(8,128)S(1)}, f32[4,64,512]{2,1,0:T(8,128)S(1)}, f32[8,4,64]{2,1,0:T(4,128)S(1)}, f32[8,4,64,512]{3,2,1,0:T(8...) while((s32[]{:T(128)}, f32[4,64,512]{2,1,0:T(8,128)S(1)}, ...), condition=%wide.region_19.19_spmd.clone.clone, body=%wide.region_15.18_spmd.clone.clone.sunk | while | flops 84529344 | bytes 8700445 | solution.py:77
  4198.1 227.5 %while.240 = (s32[]{:T(128)}, f32[4,64,512]{2,1,0:T(8,128)S(1)}, f32[4,64,512]{2,1,0:T(8,128)S(1)}, f32[8,16,4,512]{3,2,1,0:T(4,128)}, f32[8,16,4,512]{3,2,1,0:T...) while((s32[]{:T(128)}, f32[4,64,512]{2,1,0:T(8,128)S(1)}, ...), condition=%wide.region_29.29_spmd.clone.clone, body=%wide.region_20.28_spmd.clone.clone.sunk | while | flops 230158336 | bytes 13886109 | solution.py:77
  4503.4 11.9 fusion.214
  4515.4 12.1 fusion.215
  4528.2 11.5 fusion.176
  4549.6 12.8 fusion.212
  4562.4 13.4 fusion.211
  4575.8 14.4 fusion.213
  4600.6 24.5 all-reduce.5
  4637.5 38.2 reduce-scatter.15.cloned.1.call-done
  4675.7 55.0 %reduce-scatter.19.cloned.1.call-done = f32[256,512]{1,0:T(8,128)} async-done(((f32[2048,512]{1,0:T(8,128)}), f32[256,512]{1,0:T(8,128)}) %reduce-scatter.19.cloned.1.call-update) | async-done | bytes 524304 | tf_op jit(solution)/shard_map/reduce_scatter | solution.py:239
  4730.7 91.3 %reduce-scatter.25.cloned.1.call-done = f32[256,1408]{1,0:T(8,128)} async-done(((f32[2048,1408]{1,0:T(8,128)}), f32[256,1408]{1,0:T(8,128)}) %reduce-scatter.25.cloned.1.call-update) | async-done | bytes 1441808 | tf_op jit(solution)/shard_map/reduce_scatter | solution.py:246
  4822.0 91.1 %reduce-scatter.27.cloned.1.call-done = f32[256,1408]{1,0:T(8,128)} async-done(((f32[2048,1408]{1,0:T(8,128)}), f32[256,1408]{1,0:T(8,128)}) %reduce-scatter.27.cloned.1.call-update) | async-done | bytes 1441808 | tf_op jit(solution)/shard_map/reduce_scatter | solution.py:247
  4913.0 91.0 %reduce-scatter.29.cloned.1.call-done = f32[1408,256]{1,0:T(8,128)} async-done(((f32[1408,2048]{1,0:T(8,128)}), f32[1408,256]{1,0:T(8,128)}) %reduce-scatter.29.cloned.1.call-update) | async-done | bytes 1441808 | tf_op jit(solution)/shard_map/reduce_scatter | solution.py:248
  (5807 shorter events, 4031.2 us)
Async XLA Ops:
  7.2 89.6 %copy-start = (bf16[2048,16]{0,1:T(8,128)(2,1)S(1)}, bf16[2048,16]{0,1:T(8,128)(2,1)}, u32[]{:S(2)}) copy-start(bf16[2048,16]{0,1:T(8,128)(2,1)} %param.32) | copy-start | bytes 196612
  7.2 85.9 %all-gather.3.cloned.1.call-start = ((), (), s32[]{:S(2)}) async-start(), calls=%async_computation.10 | async-start | bytes 5242880 | tf_op jit(solution)/shard_map/all_gather | solution.py:116
  7.9 92.3 %copy-start.33 = (bf16[16,256]{1,0:T(8,128)(2,1)S(1)}, bf16[16,256]{1,0:T(8,128)(2,1)}, u32[]{:S(2)}) copy-start(bf16[16,256]{1,0:T(8,128)(2,1)} %param.33) | copy-start | bytes 24580
  7.9 92.3 %copy-start.41 = (f32[256]{0:T(256)S(1)}, f32[256]{0:T(256)}, u32[]{:S(2)}) copy-start(f32[256]{0:T(256)} %param.34) | copy-start | bytes 3076
  8.0 1062.7 %all-gather.5.cloned.1.call-start = ((), (), s32[]{:S(2)}) async-start(), calls=%async_computation.12 | async-start | bytes 5242880 | tf_op jit(solution)/shard_map/all_gather | solution.py:117
  8.7 1389.4 %all-reduce.8.cloned.1.call-start = ((), (), s32[]{:S(2)}) async-start(), calls=%async_computation.13 | async-start | bytes 16777216 | tf_op jit(solution)/shard_map/psum | solution.py:175
  96.7 81.1 %copy-start.28 = (f32[1024]{0:T(1024)}, f32[1024]{0:T(1024)S(1)}, u32[]{:S(2)}) copy-start(f32[1024]{0:T(1024)S(1)} %fusion.192) | copy-start | bytes 12292
  100.2 21.8 copy-start.24
  132.9 9.3 copy-start.2
  168.6 9.3 copy-start.3
  1003.5 9.3 copy-start.19
  1003.7 9.0 copy-start.10
  1003.7 9.0 slice-start
  1020.1 11.9 copy-start.4
  1020.1 11.9 copy-start.35
  1032.0 14.3 copy-start.23
  1046.2 14.1 copy-start.1
  1060.4 10.3 copy-start.30
  1086.9 10.8 copy-start.44
  1086.9 10.8 copy-start.43
  1108.5 3519.2 %reduce-scatter.13.cloned.1.call-start = ((), (), s32[]{:S(2)}) async-start(), calls=%async_computation.11 | async-start | bytes 5242880 | tf_op jit(solution)/shard_map/reduce_scatter | solution.py:157
  1123.3 3512.8 %reduce-scatter.31.cloned.1.call-start = ((), (), s32[]{:S(2)}) async-start(), calls=%async_computation.22 | async-start | bytes 147456
  1398.1 9.0 copy-start.9
  1398.1 10.2 copy-start.18
  1398.1 19.0 slice-start.2
  1408.3 8.8 slice-start.3
  1432.3 10.9 copy-start.32
  1443.2 8.7 copy-start.11
  1473.6 2962.6 %copy-start.34 = (bf16[16,256]{1,0:T(8,128)(2,1)S(1)}, bf16[16,256]{1,0:T(8,128)(2,1)}, u32[]{:S(2)}) copy-start(bf16[16,256]{1,0:T(8,128)(2,1)} %param.33) | copy-start | bytes 24580
  4431.7 8.6 copy-start.29
  4431.7 12.6 copy-start.36
  4436.9 15.6 copy-start.21
  4440.2 197.3 %reduce-scatter.21.cloned.1.call-start = ((), (), s32[]{:S(2)}) async-start(), calls=%async_computation.17 | async-start | bytes 147456 | tf_op jit(solution)/shard_map/reduce_scatter | solution.py:240
  4444.3 193.3 %reduce-scatter.23.cloned.1.call-start = ((), (), s32[]{:S(2)}) async-start(), calls=%async_computation.18 | async-start | bytes 4718592 | tf_op jit(solution)/shard_map/reduce_scatter | solution.py:244
  4452.5 185.1 %reduce-scatter.17.cloned.1.call-start = ((), (), s32[]{:S(2)}) async-start(), calls=%async_computation.15 | async-start | bytes 4718592 | tf_op jit(solution)/shard_map/reduce_scatter | solution.py:238
  4472.5 203.2 %reduce-scatter.15.cloned.1.call-start = ((), (), s32[]{:S(2)}) async-start(), calls=%async_computation.14 | async-start | bytes 4718592 | tf_op jit(solution)/shard_map/reduce_scatter | solution.py:237
  4492.8 237.9 %reduce-scatter.19.cloned.1.call-start = ((), (), s32[]{:S(2)}) async-start(), calls=%async_computation.16 | async-start | bytes 4718592 | tf_op jit(solution)/shard_map/reduce_scatter | solution.py:239
  4503.3 318.6 %reduce-scatter.25.cloned.1.call-start = ((), (), s32[]{:S(2)}) async-start(), calls=%async_computation.19 | async-start | bytes 12976128 | tf_op jit(solution)/shard_map/reduce_scatter | solution.py:246
  4515.3 397.7 %reduce-scatter.27.cloned.1.call-start = ((), (), s32[]{:S(2)}) async-start(), calls=%async_computation.20 | async-start | bytes 12976128 | tf_op jit(solution)/shard_map/reduce_scatter | solution.py:247
  4527.5 476.5 %reduce-scatter.29.cloned.1.call-start = ((), (), s32[]{:S(2)}) async-start(), calls=%async_computation.21 | async-start | bytes 12976128 | tf_op jit(solution)/shard_map/reduce_scatter | solution.py:248
  4539.7 9.9 copy-start.37
  4549.6 12.8 copy-start.15
  4562.4 13.4 copy-start.17
  4575.8 14.4 copy-start.8
  4575.8 14.4 copy-start.22
  4590.2 10.4 copy-start.27
  4590.2 10.4 copy-start.40
  4590.2 36.2 copy-start.26
  (16 other events, 81.0 us)
Sparse Core Ops, SparseCore 0:
  9.6 83.4 all-gather.2
  94.6 79.2 all-gather.4
  1108.6 289.5 all-reduce.7
  1400.3 75.7 reduce-scatter.12
  4440.3 32.6 reduce-scatter.30
  4476.5 33.5 reduce-scatter.20
  4514.0 51.1 reduce-scatter.22
  4569.1 51.4 reduce-scatter.16
  4624.5 51.1 reduce-scatter.14
  4679.5 51.1 reduce-scatter.18
  4734.8 87.1 reduce-scatter.24
  4825.9 87.1 reduce-scatter.26
  4917.1 86.8 reduce-scatter.28
where the time goes:
time: 5100 us; the launch traced here: 5010 us
  matrix products  2080 us (41%)
  local copies, waits for them, and re-layouts  1160 us (23%)
  other arithmetic  985 us (19%)
  waiting for transfers between devices  725 us (14%)
    dot_general x256, matrix products, piece_step(): jnp.einsum('cso,sio->csi', query_rows, key_slot_state, precision=HIGH_PRE...  357 us
    dot_general x256, matrix products, piece_step(): jnp.einsum('thd,jhd->htj', query_rows, key_row_block, precision=HIGH_PREC...  286 us
    psum x1, waiting for transfers between devices, local(): grad_normed_mlp = lax.psum(partial_grad, 'mp')  275 us
    dot_general x256, matrix products, piece_step(): jnp.einsum('eoq,eon->oqn', carried_state, value_row_block, precision=HIGH...  261 us
    dynamic_slice x448, local copies, waits for them, and re-layouts, slot_block(): states, output_rows = lax.scan(piece_step, states, pieces)  258 us
    dot_general x192, matrix products, piece_step(): jnp.einsum('lwe,wez->lwz', attention_probabilities * jnp.exp(running_tota...  236 us
    dynamic_update_slice x320, other arithmetic, slot_block(): states, output_rows = lax.scan(piece_step, states, pieces)  221 us
    dot_general x256, matrix products, piece_step(): jnp.einsum('eoq,eon->oqn', carried_state, key_row_block, precision=HIGH_P...  204 us

commit v1 on v0

--- a/solution.py
+++ b/solution.py
@@ -3,6 +3,7 @@
 import jax.numpy as jnp
 from jax import lax
 from jax.sharding import PartitionSpec as P
+from jax.lax import ppermute, psum
 
 HEADS = 4
 BLOCK = 128
@@ -11,6 +12,15 @@
 HIGH_PRECISION = lax.Precision.HIGHEST
 CONTRACT_ROWS = (((0,), (0,)), ((), ()))
 CONTRACT_COLS = (((1,), (1,)), ((), ()))
+
+
+def carry_strings(v0):
+    ndev = psum(1, "mp")
+    block_next = v0
+    for idx in [[(k, k ^ nth) for k in range(ndev)] for nth in (1, 2, 4, 8, 16) if nth < ndev]:
+        parts_out = ppermute(block_next, "mp", idx)
+        block_next = block_next + parts_out
+    return block_next
 
 
 def rms_norm(values, gain):
@@ -172,7 +182,7 @@
     grad_gate = rows_product(mlp_low, grad_gate_low)
     grad_up = rows_product(mlp_low, grad_up_low)
     partial_grad = cols_product(grad_gate_low, w_gate) + cols_product(grad_up_low, w_up)
-    grad_normed_mlp = lax.psum(partial_grad, "mp")
+    grad_normed_mlp = carry_strings(partial_grad)
     grad_res_mlp, grad_mlp_gain = pull_second(grad_normed_mlp)
     grad_hidden = grad_output + grad_res_mlp
 

time: 5100 us -> 5420 us (1.063)
  waiting for transfers between devices: 725 us -> 1040 us
    ppermute x0 -> x2, waiting for transfers between devices: none -> 597 us  [carry_strings(): parts_out = ppermute(block_next, 'mp', idx)]
    psum x1 -> x0, waiting for transfers between devices: 275 us -> none  [local(): grad_normed_mlp = lax.psum(partial_grad, 'mp')]
    reduce_scatter x1, waiting for transfers between devices: 91 us -> 0.01 us  [local(): lax.psum_scatter(grad_down, 'dp', scatter_dimension=1, tiled=True)]
    dot_general x256, matrix products: 286 us -> 227 us  [piece_step(): jnp.einsum('thd,jhd->htj', query_rows, key_row_block, precision=HIGH_PREC...]
    dot_general x256, matrix products: 261 us -> 319 us  [piece_step(): jnp.einsum('eoq,eon->oqn', carried_state, value_row_block, precision=HIGH...]
    dot_general x256, matrix products: 204 us -> 147 us  [piece_step(): jnp.einsum('eoq,eon->oqn', carried_state, key_row_block, precision=HIGH_P...]
    dot_general x192, matrix products: 175 us -> 232 us  [piece_step(): jnp.einsum('htj,jhd->thd', mixing, value_row_block, precision=HIGH_PRECIS...]
    reduce_scatter x1, waiting for transfers between devices: 0.01 us -> 55.1 us  [local(): lax.psum_scatter(grad_wout, 'dp', scatter_dimension=0, tiled=True)]
where the time goes in v1:
time: 5420 us; the launch traced here: 5340 us
  matrix products  2080 us (38%)
  local copies, waits for them, and re-layouts  1140 us (21%)
  waiting for transfers between devices  1040 us (19%)
  other arithmetic  1010 us (19%)
    ppermute x2, waiting for transfers between devices, carry_strings(): parts_out = ppermute(block_next, 'mp', idx)  597 us
    dot_general x256, matrix products, piece_step(): jnp.einsum('cso,sio->csi', query_rows, key_slot_state, precision=HIGH_PRE...  357 us
    dot_general x256, matrix products, piece_step(): jnp.einsum('eoq,eon->oqn', carried_state, value_row_block, precision=HIGH...  319 us
    dynamic_slice x448, local copies, waits for them, and re-layouts, slot_block(): states, output_rows = lax.scan(piece_step, states, pieces)  257 us
    dot_general x192, matrix products, piece_step(): jnp.einsum('lwe,wez->lwz', attention_probabilities * jnp.exp(running_tota...  238 us
    dot_general x192, matrix products, piece_step(): jnp.einsum('htj,jhd->thd', mixing, value_row_block, precision=HIGH_PRECIS...  232 us
    dot_general x256, matrix products, piece_step(): jnp.einsum('thd,jhd->htj', query_rows, key_row_block, precision=HIGH_PREC...  227 us
    dynamic_update_slice x320, other arithmetic, slot_block(): states, output_rows = lax.scan(piece_step, states, pieces)  223 us

profile of v1, /device:TPU:0, one launch (start us, length us, event | category | flops | bytes accessed | tf_op | source)
XLA Modules:
  0.0 5336.6 jit_solution(3421227339502219328)
XLA Ops:
  11.3 81.8 %all-gather.3.cloned.1.call-done = bf16[1024,2048]{1,0:T(8,128)(2,1)} async-done(((bf16[256,2048]{1,0:T(8,128)(2,1)}), bf16[1024,2048]{1,0:T(8,128)(2,1)}) %all-gather.3.cloned.1.call-update) | async-done | bytes 4194320 | tf_op jit(solution)/shard_map/all_gather | solution.py:126
  104.5 15.1 convert_convert_fusion
  139.8 15.4 fusion.174
  175.5 15.4 fusion.173
  216.6 765.9 %while.238 = (s32[]{:T(128)}, f32[4,64,512]{2,1,0:T(8,128)S(1)}, f32[4,64,512]{2,1,0:T(8,128)}, f32[8,128,4,512]{3,2,1,0:T(4,128)}, f32[8,4,64,512]{3,2,1,0:T(8,...) while((s32[]{:T(128)}, f32[4,64,512]{2,1,0:T(8,128)S(1)}, ...), condition=%wide.region_7.8_spmd.clone.clone, body=%wide.region_1.7_spmd.clone.clone.sunk | while | flops 115744832 | bytes 22997152 | solution.py:102
  224.0 83.1 %while.241 = (s32[]{:T(128)}, f32[4,64,512]{2,1,0:T(8,128)S(1)}, f32[4,64,512]{2,1,0:T(8,128)S(1)}, f32[8,16,4,512]{3,2,1,0:T(4,128)}, f32[8,16,4,64]{3,2,1,0:T(...) while((s32[]{:T(128)}, f32[4,64,512]{2,1,0:T(8,128)S(1)}, ...), condition=%wide.region_6.6_spmd.clone, body=%wide.region_2.5_spmd.clone.sunk | while | flops 115744832 | bytes 5891725 | solution.py:87
  319.6 83.1 %while.241 = (s32[]{:T(128)}, f32[4,64,512]{2,1,0:T(8,128)S(1)}, f32[4,64,512]{2,1,0:T(8,128)S(1)}, f32[8,16,4,512]{3,2,1,0:T(4,128)}, f32[8,16,4,64]{3,2,1,0:T(...) while((s32[]{:T(128)}, f32[4,64,512]{2,1,0:T(8,128)S(1)}, ...), condition=%wide.region_6.6_spmd.clone, body=%wide.region_2.5_spmd.clone.sunk | while | flops 115744832 | bytes 5891725 | solution.py:87
  415.3 83.1 %while.241 = (s32[]{:T(128)}, f32[4,64,512]{2,1,0:T(8,128)S(1)}, f32[4,64,512]{2,1,0:T(8,128)S(1)}, f32[8,16,4,512]{3,2,1,0:T(4,128)}, f32[8,16,4,64]{3,2,1,0:T(...) while((s32[]{:T(128)}, f32[4,64,512]{2,1,0:T(8,128)S(1)}, ...), condition=%wide.region_6.6_spmd.clone, body=%wide.region_2.5_spmd.clone.sunk | while | flops 115744832 | bytes 5891725 | solution.py:87
  511.0 83.1 %while.241 = (s32[]{:T(128)}, f32[4,64,512]{2,1,0:T(8,128)S(1)}, f32[4,64,512]{2,1,0:T(8,128)S(1)}, f32[8,16,4,512]{3,2,1,0:T(4,128)}, f32[8,16,4,64]{3,2,1,0:T(...) while((s32[]{:T(128)}, f32[4,64,512]{2,1,0:T(8,128)S(1)}, ...), condition=%wide.region_6.6_spmd.clone, body=%wide.region_2.5_spmd.clone.sunk | while | flops 115744832 | bytes 5891725 | solution.py:87
  606.7 83.1 %while.241 = (s32[]{:T(128)}, f32[4,64,512]{2,1,0:T(8,128)S(1)}, f32[4,64,512]{2,1,0:T(8,128)S(1)}, f32[8,16,4,512]{3,2,1,0:T(4,128)}, f32[8,16,4,64]{3,2,1,0:T(...) while((s32[]{:T(128)}, f32[4,64,512]{2,1,0:T(8,128)S(1)}, ...), condition=%wide.region_6.6_spmd.clone, body=%wide.region_2.5_spmd.clone.sunk | while | flops 115744832 | bytes 5891725 | solution.py:87
  702.4 83.1 %while.241 = (s32[]{:T(128)}, f32[4,64,512]{2,1,0:T(8,128)S(1)}, f32[4,64,512]{2,1,0:T(8,128)S(1)}, f32[8,16,4,512]{3,2,1,0:T(4,128)}, f32[8,16,4,64]{3,2,1,0:T(...) while((s32[]{:T(128)}, f32[4,64,512]{2,1,0:T(8,128)S(1)}, ...), condition=%wide.region_6.6_spmd.clone, body=%wide.region_2.5_spmd.clone.sunk | while | flops 115744832 | bytes 5891725 | solution.py:87
  798.1 83.1 %while.241 = (s32[]{:T(128)}, f32[4,64,512]{2,1,0:T(8,128)S(1)}, f32[4,64,512]{2,1,0:T(8,128)S(1)}, f32[8,16,4,512]{3,2,1,0:T(4,128)}, f32[8,16,4,64]{3,2,1,0:T(...) while((s32[]{:T(128)}, f32[4,64,512]{2,1,0:T(8,128)S(1)}, ...), condition=%wide.region_6.6_spmd.clone, body=%wide.region_2.5_spmd.clone.sunk | while | flops 115744832 | bytes 5891725 | solution.py:87
  894.0 83.1 %while.241 = (s32[]{:T(128)}, f32[4,64,512]{2,1,0:T(8,128)S(1)}, f32[4,64,512]{2,1,0:T(8,128)S(1)}, f32[8,16,4,512]{3,2,1,0:T(4,128)}, f32[8,16,4,64]{3,2,1,0:T(...) while((s32[]{:T(128)}, f32[4,64,512]{2,1,0:T(8,128)S(1)}, ...), condition=%wide.region_6.6_spmd.clone, body=%wide.region_2.5_spmd.clone.sunk | while | flops 115744832 | bytes 5891725 | solution.py:87
  1016.7 14.2 multiply_reduce_fusion.6
  1031.8 15.0 fusion.209
  1055.3 16.0 multiply_convert_fusion.7
  1095.0 182.1 %collective-permute-done = f32[1024,2048]{1,0:T(8,128)} collective-permute-done((f32[1024,2048]{1,0:T(8,128)S(1)}, f32[1024,2048]{1,0:T(8,128)}, u32[]{:S(2)}, u32[]{:S(2)}) %collective-permute-start) | collective-permute-done | bytes 8388640 | tf_op jit(solution)/shard_map/ppermute | solution.py:21
  1304.0 414.6 %collective-permute-done.1 = f32[1024,2048]{1,0:T(8,128)} collective-permute-done((f32[1024,2048]{1,0:T(8,128)}, f32[1024,2048]{1,0:T(8,128)}, u32[]{:S(2)}, u32[]{:S(2)}) %collective-permute-start.1) | collective-permute-done | bytes 8388640 | tf_op jit(solution)/shard_map/ppermute | solution.py:21
  1729.5 14.6 fusion.204
  1744.2 15.1 multiply_reduce_fusion.1
  1800.6 2956.7 %while.236 = (s32[]{:T(128)}, f32[4,64,512]{2,1,0:T(8,128)S(1)}, f32[4,64,512]{2,1,0:T(8,128)S(1)}, f32[8,128,4,512]{3,2,1,0:T(4,128)}, f32[8,128,4,512]{3,2,1,0...) while((s32[]{:T(128)}, f32[4,64,512]{2,1,0:T(8,128)S(1)}, ...), condition=%wide.region_29.30_spmd, body=%wide.region_13.0_spmd.sunk | while | flops 314950080 | bytes 50764040 | solution.py:102
  1817.3 117.3 %while.239 = (s32[]{:T(128)}, f32[4,64,512]{2,1,0:T(8,128)S(1)}, f32[4,64,512]{2,1,0:T(8,128)S(1)}, f32[8,4,64]{2,1,0:T(4,128)S(1)}, f32[8,4,64,512]{3,2,1,0:T(8...) while((s32[]{:T(128)}, f32[4,64,512]{2,1,0:T(8,128)S(1)}, ...), condition=%wide.region_18.18_spmd.clone.clone, body=%wide.region_14.17_spmd.clone.clone.sunk | while | flops 84529344 | bytes 8696389 | solution.py:87
  1936.9 227.2 %while.240 = (s32[]{:T(128)}, f32[4,64,512]{2,1,0:T(8,128)S(1)}, f32[4,64,512]{2,1,0:T(8,128)S(1)}, f32[8,16,4,512]{3,2,1,0:T(4,128)}, f32[8,16,4,512]{3,2,1,0:T...) while((s32[]{:T(128)}, f32[4,64,512]{2,1,0:T(8,128)S(1)}, ...), condition=%wide.region_28.28_spmd.clone.clone, body=%wide.region_19.27_spmd.clone.clone.sunk | while | flops 230158336 | bytes 13886109 | solution.py:87
  2186.8 117.3 %while.239 = (s32[]{:T(128)}, f32[4,64,512]{2,1,0:T(8,128)S(1)}, f32[4,64,512]{2,1,0:T(8,128)S(1)}, f32[8,4,64]{2,1,0:T(4,128)S(1)}, f32[8,4,64,512]{3,2,1,0:T(8...) while((s32[]{:T(128)}, f32[4,64,512]{2,1,0:T(8,128)S(1)}, ...), condition=%wide.region_18.18_spmd.clone.clone, body=%wide.region_14.17_spmd.clone.clone.sunk | while | flops 84529344 | bytes 8696389 | solution.py:87
  2306.5 227.2 %while.240 = (s32[]{:T(128)}, f32[4,64,512]{2,1,0:T(8,128)S(1)}, f32[4,64,512]{2,1,0:T(8,128)S(1)}, f32[8,16,4,512]{3,2,1,0:T(4,128)}, f32[8,16,4,512]{3,2,1,0:T...) while((s32[]{:T(128)}, f32[4,64,512]{2,1,0:T(8,128)S(1)}, ...), condition=%wide.region_28.28_spmd.clone.clone, body=%wide.region_19.27_spmd.clone.clone.sunk | while | flops 230158336 | bytes 13886109 | solution.py:87
  2556.4 117.3 %while.239 = (s32[]{:T(128)}, f32[4,64,512]{2,1,0:T(8,128)S(1)}, f32[4,64,512]{2,1,0:T(8,128)S(1)}, f32[8,4,64]{2,1,0:T(4,128)S(1)}, f32[8,4,64,512]{3,2,1,0:T(8...) while((s32[]{:T(128)}, f32[4,64,512]{2,1,0:T(8,128)S(1)}, ...), condition=%wide.region_18.18_spmd.clone.clone, body=%wide.region_14.17_spmd.clone.clone.sunk | while | flops 84529344 | bytes 8696389 | solution.py:87
  2676.0 227.2 %while.240 = (s32[]{:T(128)}, f32[4,64,512]{2,1,0:T(8,128)S(1)}, f32[4,64,512]{2,1,0:T(8,128)S(1)}, f32[8,16,4,512]{3,2,1,0:T(4,128)}, f32[8,16,4,512]{3,2,1,0:T...) while((s32[]{:T(128)}, f32[4,64,512]{2,1,0:T(8,128)S(1)}, ...), condition=%wide.region_28.28_spmd.clone.clone, body=%wide.region_19.27_spmd.clone.clone.sunk | while | flops 230158336 | bytes 13886109 | solution.py:87
  2925.9 117.3 %while.239 = (s32[]{:T(128)}, f32[4,64,512]{2,1,0:T(8,128)S(1)}, f32[4,64,512]{2,1,0:T(8,128)S(1)}, f32[8,4,64]{2,1,0:T(4,128)S(1)}, f32[8,4,64,512]{3,2,1,0:T(8...) while((s32[]{:T(128)}, f32[4,64,512]{2,1,0:T(8,128)S(1)}, ...), condition=%wide.region_18.18_spmd.clone.clone, body=%wide.region_14.17_spmd.clone.clone.sunk | while | flops 84529344 | bytes 8696389 | solution.py:87
  3045.6 227.2 %while.240 = (s32[]{:T(128)}, f32[4,64,512]{2,1,0:T(8,128)S(1)}, f32[4,64,512]{2,1,0:T(8,128)S(1)}, f32[8,16,4,512]{3,2,1,0:T(4,128)}, f32[8,16,4,512]{3,2,1,0:T...) while((s32[]{:T(128)}, f32[4,64,512]{2,1,0:T(8,128)S(1)}, ...), condition=%wide.region_28.28_spmd.clone.clone, body=%wide.region_19.27_spmd.clone.clone.sunk | while | flops 230158336 | bytes 13886109 | solution.py:87
  3295.5 117.3 %while.239 = (s32[]{:T(128)}, f32[4,64,512]{2,1,0:T(8,128)S(1)}, f32[4,64,512]{2,1,0:T(8,128)S(1)}, f32[8,4,64]{2,1,0:T(4,128)S(1)}, f32[8,4,64,512]{3,2,1,0:T(8...) while((s32[]{:T(128)}, f32[4,64,512]{2,1,0:T(8,128)S(1)}, ...), condition=%wide.region_18.18_spmd.clone.clone, body=%wide.region_14.17_spmd.clone.clone.sunk | while | flops 84529344 | bytes 8696389 | solution.py:87
  3415.1 227.2 %while.240 = (s32[]{:T(128)}, f32[4,64,512]{2,1,0:T(8,128)S(1)}, f32[4,64,512]{2,1,0:T(8,128)S(1)}, f32[8,16,4,512]{3,2,1,0:T(4,128)}, f32[8,16,4,512]{3,2,1,0:T...) while((s32[]{:T(128)}, f32[4,64,512]{2,1,0:T(8,128)S(1)}, ...), condition=%wide.region_28.28_spmd.clone.clone, body=%wide.region_19.27_spmd.clone.clone.sunk | while | flops 230158336 | bytes 13886109 | solution.py:87
  3665.0 117.3 %while.239 = (s32[]{:T(128)}, f32[4,64,512]{2,1,0:T(8,128)S(1)}, f32[4,64,512]{2,1,0:T(8,128)S(1)}, f32[8,4,64]{2,1,0:T(4,128)S(1)}, f32[8,4,64,512]{3,2,1,0:T(8...) while((s32[]{:T(128)}, f32[4,64,512]{2,1,0:T(8,128)S(1)}, ...), condition=%wide.region_18.18_spmd.clone.clone, body=%wide.region_14.17_spmd.clone.clone.sunk | while | flops 84529344 | bytes 8696389 | solution.py:87
  3784.7 227.2 %while.240 = (s32[]{:T(128)}, f32[4,64,512]{2,1,0:T(8,128)S(1)}, f32[4,64,512]{2,1,0:T(8,128)S(1)}, f32[8,16,4,512]{3,2,1,0:T(4,128)}, f32[8,16,4,512]{3,2,1,0:T...) while((s32[]{:T(128)}, f32[4,64,512]{2,1,0:T(8,128)S(1)}, ...), condition=%wide.region_28.28_spmd.clone.clone, body=%wide.region_19.27_spmd.clone.clone.sunk | while | flops 230158336 | bytes 13886109 | solution.py:87
  4034.6 117.3 %while.239 = (s32[]{:T(128)}, f32[4,64,512]{2,1,0:T(8,128)S(1)}, f32[4,64,512]{2,1,0:T(8,128)S(1)}, f32[8,4,64]{2,1,0:T(4,128)S(1)}, f32[8,4,64,512]{3,2,1,0:T(8...) while((s32[]{:T(128)}, f32[4,64,512]{2,1,0:T(8,128)S(1)}, ...), condition=%wide.region_18.18_spmd.clone.clone, body=%wide.region_14.17_spmd.clone.clone.sunk | while | flops 84529344 | bytes 8696389 | solution.py:87
  4154.2 227.2 %while.240 = (s32[]{:T(128)}, f32[4,64,512]{2,1,0:T(8,128)S(1)}, f32[4,64,512]{2,1,0:T(8,128)S(1)}, f32[8,16,4,512]{3,2,1,0:T(4,128)}, f32[8,16,4,512]{3,2,1,0:T...) while((s32[]{:T(128)}, f32[4,64,512]{2,1,0:T(8,128)S(1)}, ...), condition=%wide.region_28.28_spmd.clone.clone, body=%wide.region_19.27_spmd.clone.clone.sunk | while | flops 230158336 | bytes 13886109 | solution.py:87
  4404.1 117.3 %while.239 = (s32[]{:T(128)}, f32[4,64,512]{2,1,0:T(8,128)S(1)}, f32[4,64,512]{2,1,0:T(8,128)S(1)}, f32[8,4,64]{2,1,0:T(4,128)S(1)}, f32[8,4,64,512]{3,2,1,0:T(8...) while((s32[]{:T(128)}, f32[4,64,512]{2,1,0:T(8,128)S(1)}, ...), condition=%wide.region_18.18_spmd.clone.clone, body=%wide.region_14.17_spmd.clone.clone.sunk | while | flops 84529344 | bytes 8696389 | solution.py:87
  4523.8 227.2 %while.240 = (s32[]{:T(128)}, f32[4,64,512]{2,1,0:T(8,128)S(1)}, f32[4,64,512]{2,1,0:T(8,128)S(1)}, f32[8,16,4,512]{3,2,1,0:T(4,128)}, f32[8,16,4,512]{3,2,1,0:T...) while((s32[]{:T(128)}, f32[4,64,512]{2,1,0:T(8,128)S(1)}, ...), condition=%wide.region_28.28_spmd.clone.clone, body=%wide.region_19.27_spmd.clone.clone.sunk | while | flops 230158336 | bytes 13886109 | solution.py:87
  4793.7 12.1 fusion.214
  4878.8 14.7 fusion.213
  4893.6 15.2 fusion.212
  4908.8 13.6 fusion.211
  4932.5 24.5 all-reduce.5
  4965.5 52.6 reduce-scatter.27.cloned.1.call-done
  5018.1 91.2 %reduce-scatter.25.cloned.1.call-done = f32[256,1408]{1,0:T(8,128)} async-done(((f32[2048,1408]{1,0:T(8,128)}), f32[256,1408]{1,0:T(8,128)}) %reduce-scatter.25.cloned.1.call-update) | async-done | bytes 1441808 | tf_op jit(solution)/shard_map/reduce_scatter | solution.py:256
  5109.3 55.1 %reduce-scatter.23.cloned.1.call-done = f32[256,512]{1,0:T(8,128)} async-done(((f32[2048,512]{1,0:T(8,128)}), f32[256,512]{1,0:T(8,128)}) %reduce-scatter.23.cloned.1.call-update) | async-done | bytes 524304 | tf_op jit(solution)/shard_map/reduce_scatter | solution.py:254
  5164.4 55.0 %reduce-scatter.19.cloned.1.call-done = f32[256,512]{1,0:T(8,128)} async-done(((f32[2048,512]{1,0:T(8,128)}), f32[256,512]{1,0:T(8,128)}) %reduce-scatter.19.cloned.1.call-update) | async-done | bytes 524304 | tf_op jit(solution)/shard_map/reduce_scatter | solution.py:249
  5219.4 55.1 %reduce-scatter.17.cloned.1.call-done = f32[256,512]{1,0:T(8,128)} async-done(((f32[2048,512]{1,0:T(8,128)}), f32[256,512]{1,0:T(8,128)}) %reduce-scatter.17.cloned.1.call-update) | async-done | bytes 524304 | tf_op jit(solution)/shard_map/reduce_scatter | solution.py:248
  5274.6 55.0 %reduce-scatter.15.cloned.1.call-done = f32[256,512]{1,0:T(8,128)} async-done(((f32[2048,512]{1,0:T(8,128)}), f32[256,512]{1,0:T(8,128)}) %reduce-scatter.15.cloned.1.call-update) | async-done | bytes 524304 | tf_op jit(solution)/shard_map/reduce_scatter | solution.py:247
  (5833 shorter events, 4055.6 us)
Async XLA Ops:
  7.2 89.5 %copy-start = (bf16[2048,16]{0,1:T(8,128)(2,1)S(1)}, bf16[2048,16]{0,1:T(8,128)(2,1)}, u32[]{:S(2)}) copy-start(bf16[2048,16]{0,1:T(8,128)(2,1)} %param.32) | copy-start | bytes 196612
  7.2 85.9 %all-gather.3.cloned.1.call-start = ((), (), s32[]{:S(2)}) async-start(), calls=%async_computation.10 | async-start | bytes 5242880 | tf_op jit(solution)/shard_map/all_gather | solution.py:126
  7.9 92.3 %copy-start.33 = (bf16[16,256]{1,0:T(8,128)(2,1)S(1)}, bf16[16,256]{1,0:T(8,128)(2,1)}, u32[]{:S(2)}) copy-start(bf16[16,256]{1,0:T(8,128)(2,1)} %param.33) | copy-start | bytes 24580
  7.9 92.3 %copy-start.41 = (f32[256]{0:T(256)S(1)}, f32[256]{0:T(256)}, u32[]{:S(2)}) copy-start(f32[256]{0:T(256)} %param.34) | copy-start | bytes 3076
  8.0 1047.3 %all-gather.5.cloned.1.call-start = ((), (), s32[]{:S(2)}) async-start(), calls=%async_computation.12 | async-start | bytes 5242880 | tf_op jit(solution)/shard_map/all_gather | solution.py:127
  8.7 4848.6 %reduce-scatter.13.cloned.1.call-start = ((), (), s32[]{:S(2)}) async-start(), calls=%async_computation.11 | async-start | bytes 5242880 | tf_op jit(solution)/shard_map/reduce_scatter | solution.py:167
  96.7 78.8 %copy-start.28 = (f32[1024]{0:T(1024)}, f32[1024]{0:T(1024)S(1)}, u32[]{:S(2)}) copy-start(f32[1024]{0:T(1024)S(1)} %fusion.192) | copy-start | bytes 12292
  100.2 19.4 copy-start.24
  130.5 9.3 copy-start.3
  987.8 9.6 copy-start.19
  988.1 9.4 copy-start.11
  1004.8 11.9 copy-start.5
  1004.8 11.9 copy-start.35
  1016.7 14.3 copy-start.23
  1031.0 15.8 copy-start.1
  1031.0 15.8 slice-start.8
  1031.8 15.0 copy-start.14
  1031.8 15.0 slice-start.9
  1071.2 10.8 copy-start.44
  1071.2 221.9 %copy-start.43 = (bf16[1024,1408]{1,0:T(8,128)(2,1)}, bf16[1024,1408]{1,0:T(8,128)(2,1)S(1)}, u32[]{:S(2)}) copy-start(bf16[1024,1408]{1,0:T(8,128)(2,1)S(1)} %get-tuple-element.3183) | copy-start | bytes 8650756
  1095.0 182.1 %collective-permute-start = (f32[1024,2048]{1,0:T(8,128)S(1)}, f32[1024,2048]{1,0:T(8,128)}, u32[]{:S(2)}, u32[]{:S(2)}) collective-permute-start(f32[1024,2048]{1,0:T(8,128)S(1)} %convolution_add_fusion.9), channel_id=1, source_target_pairs={{0,1},{1,0},{2,3},{3,2},{4,5},{5,4},{6,7},{7,6},{8,9},{9,8},{10,11... | collective-permute-start | bytes 25165832 | tf_op jit(solution)/shard_map/ppermute | solution.py:21
  1289.0 429.6 %collective-permute-start.1 = (f32[1024,2048]{1,0:T(8,128)}, f32[1024,2048]{1,0:T(8,128)}, u32[]{:S(2)}, u32[]{:S(2)}) collective-permute-start(f32[1024,2048]{1,0:T(8,128)} %add.261), channel_id=1, source_target_pairs={{0,2},{1,3},{2,0},{3,1},{4,6},{5,7},{6,4},{7,5},{8,10},{9,11},{10,... | collective-permute-start | bytes 25165832 | tf_op jit(solution)/shard_map/ppermute | solution.py:21
  1304.0 3660.2 %reduce-scatter.31.cloned.1.call-start = ((), (), s32[]{:S(2)}) async-start(), calls=%async_computation.21 | async-start | bytes 147456
  1304.0 425.5 %copy-start.13 = (bf16[1024,2048]{1,0:T(8,128)(2,1)S(1)}, bf16[1024,2048]{1,0:T(8,128)(2,1)}, u32[]{:S(2)}) copy-start(bf16[1024,2048]{1,0:T(8,128)(2,1)} %all-gather.5.cloned.1.call-done) | copy-start | bytes 12582916
  1718.6 25.6 slice-start.2
  1729.5 14.6 slice-start.3
  1759.3 10.8 copy-start.32
  1800.6 2961.4 %copy-start.34 = (bf16[16,256]{1,0:T(8,128)(2,1)S(1)}, bf16[16,256]{1,0:T(8,128)(2,1)}, u32[]{:S(2)}) copy-start(bf16[16,256]{1,0:T(8,128)(2,1)} %param.33) | copy-start | bytes 24580
  4757.4 12.6 copy-start.31
  4762.6 19.1 copy-start.21
  4765.9 199.6 %reduce-scatter.21.cloned.1.call-start = ((), (), s32[]{:S(2)}) async-start(), calls=%async_computation.16 | async-start | bytes 147456 | tf_op jit(solution)/shard_map/reduce_scatter | solution.py:250
  4770.0 195.5 %reduce-scatter.29.cloned.1.call-start = ((), (), s32[]{:S(2)}) async-start(), calls=%async_computation.20 | async-start | bytes 12976128 | tf_op jit(solution)/shard_map/reduce_scatter | solution.py:258
  4781.7 236.3 %reduce-scatter.27.cloned.1.call-start = ((), (), s32[]{:S(2)}) async-start(), calls=%async_computation.19 | async-start | bytes 12976128 | tf_op jit(solution)/shard_map/reduce_scatter | solution.py:257
  4793.7 315.6 %reduce-scatter.25.cloned.1.call-start = ((), (), s32[]{:S(2)}) async-start(), calls=%async_computation.18 | async-start | bytes 12976128 | tf_op jit(solution)/shard_map/reduce_scatter | solution.py:256
  4805.8 358.6 %reduce-scatter.23.cloned.1.call-start = ((), (), s32[]{:S(2)}) async-start(), calls=%async_computation.17 | async-start | bytes 4718592 | tf_op jit(solution)/shard_map/reduce_scatter | solution.py:254
  4814.7 404.7 %reduce-scatter.19.cloned.1.call-start = ((), (), s32[]{:S(2)}) async-start(), calls=%async_computation.15 | async-start | bytes 4718592 | tf_op jit(solution)/shard_map/reduce_scatter | solution.py:249
  4825.3 449.2 %reduce-scatter.17.cloned.1.call-start = ((), (), s32[]{:S(2)}) async-start(), calls=%async_computation.14 | async-start | bytes 4718592 | tf_op jit(solution)/shard_map/reduce_scatter | solution.py:248
  4845.3 484.3 %reduce-scatter.15.cloned.1.call-start = ((), (), s32[]{:S(2)}) async-start(), calls=%async_computation.13 | async-start | bytes 4718592 | tf_op jit(solution)/shard_map/reduce_scatter | solution.py:247
  4857.3 11.2 slice-start.4
  4878.8 14.7 copy-start.37
  4893.6 15.2 copy-start.17
  4893.6 28.8 slice-start.6
  4908.8 13.6 copy-start.9
  4908.8 13.6 slice-start.7
  4908.8 13.6 copy-start.22
  4922.4 10.0 copy-start.26
  4922.4 10.1 copy-start.27
  4922.4 10.1 copy-start.40
  (28 other events, 143.5 us)
Sparse Core Ops, SparseCore 0:
  9.6 83.4 all-gather.2
  94.6 79.2 all-gather.4
  1304.1 254.9 reduce-scatter.12
  4766.0 32.9 reduce-scatter.30
  4802.4 33.5 reduce-scatter.20
  4839.9 86.8 reduce-scatter.28
  4930.9 87.1 reduce-scatter.26
  5022.1 87.1 reduce-scatter.24
  5113.2 51.1 reduce-scatter.22
  5168.2 51.1 reduce-scatter.18
  5223.4 51.1 reduce-scatter.16
  5278.3 51.1 reduce-scatter.14
